TPU v7x, 512 devices: a whole 4x4x16 slice. The times are simulated.
512 devices in a mesh: slab: 64 (over z, y), mem: 8 (over x, core).
Axes of the slice: x: 4, y: 4, z: 16, core: 2. Of those that a mesh axis runs over, the one named last changes fastest.
Arguments:
- present_ensemble: float32 [64, 4, 64, 512], P('mem', None, 'slab'), may hold values from -6 to 6
- delayed_ensemble: float32 [64, 2, 4, 64, 512], P('mem', None, None, 'slab'), may hold values from -6 to 6
- spreading_coefficient: float32 [64, 512], P('slab'), may hold values from 0.05 to 0.2
- transport_ratios: float32 [2, 64, 512], P(None, 'slab'), may hold values from -0.3 to 0.3
- obs_value: float32 [2, 256], replicated, may hold values from -6 to 6
- obs_error: float32 [2, 256], replicated, may hold values from 0.4 to 1.2
- obs_noise: float32 [2, 64, 256], replicated, may hold values from -6 to 6
- obs_row: int32 [2, 256], replicated, may hold values from 0 to 63
- obs_col: int32 [2, 256], replicated, may hold values from 1 to 510
- obs_field: int32 [2, 256], replicated, may hold values from 0 to 3
Outputs:
- analysis: float32 [64, 3, 4, 64, 512], P('mem', None, None, 'slab')
All inputs are finite; a program needn't handle non-finite values.
Results may differ from a plain program's by a relative error of at most 0.00011.
Values sent between devices are 32-bit elements; how exact they have to be, the bound alone decides.
A program may use at most 64 MiB of HBM per device.

v0:
```python
import jax
import jax.numpy as jnp
from jax import lax
from jax.sharding import PartitionSpec as P


def extended(shard, sides, width):
    for axis, dim in sides:
        devices, length = (lax.axis_size(axis), shard.shape[dim])
        up = [(i, (i + 1) % devices) for i in range(devices - 1)]
        down = [(j, i) for i, j in up]
        last = lax.slice_in_dim(shard, length - width, length, axis=dim)
        leading = lax.slice_in_dim(shard, 0, width, axis=dim)
        before = lax.ppermute(last, axis, up)
        after = lax.ppermute(leading, axis, down)
        shard = jnp.concatenate([before, shard, after], axis=dim)
    return shard


def propagate_ahead(present_ensemble, spreading_coefficient, transport_ratios):
    rowed = extended(present_ensemble, (("slab", 2),), 1)
    padded = jnp.pad(rowed, ((0, 0), (0, 0), (0, 0), (1, 1)))
    below = padded[:, :, 2:, 1:-1]
    above = padded[:, :, :-2, 1:-1]
    right = padded[:, :, 1:-1, 2:]
    left = padded[:, :, 1:-1, :-2]
    laplacian_operator = below + above + right + left - 4.0 * present_ensemble
    return (
        present_ensemble
        + spreading_coefficient * laplacian_operator
        - transport_ratios[0] * (below - above) * 0.5
        - transport_ratios[1] * (right - left) * 0.5
    )


def observe(level_zero, rows, cols, fields, row_start, col_start):
    members, nfield, height, width = level_zero.shape
    flat = level_zero.reshape(members, nfield * height * width)
    total = jnp.zeros((members, rows.shape[0]), jnp.float32)
    for offset, factor in ((-1, 0.25), (0, 0.5), (1, 0.25)):
        row_within = rows - row_start
        column_within = cols + offset - col_start
        valid = (
            (row_within >= 0)
            & (row_within < height)
            & (column_within >= 0)
            & (column_within < width)
        )
        index = (fields * height + jnp.clip(row_within, 0, height - 1)) * width + jnp.clip(
            column_within, 0, width - 1
        )
        picked = jnp.take(flat, index, axis=1)
        total = total + factor * jnp.where(valid[None, :], picked, 0.0)
    return total


def transform(observed, values, errors, noise):
    members = observed.shape[0]
    rescaled_values = (observed - jnp.mean(observed, axis=0, keepdims=True)) / errors[None, :]
    innovation = (values[None, :] - observed) / errors[None, :] + noise
    eye = jnp.eye(members, dtype=jnp.float32)
    system = (
        jnp.dot(
            rescaled_values,
            rescaled_values.T,
            precision=lax.Precision.HIGHEST,
            preferred_element_type=jnp.float32,
        )
        + (members - 1.0) * eye
    )
    right = jnp.dot(
        rescaled_values,
        innovation.T,
        precision=lax.Precision.HIGHEST,
        preferred_element_type=jnp.float32,
    )
    factor = jnp.linalg.cholesky(system)
    middle = lax.linalg.triangular_solve(factor, right, left_side=True, lower=True)
    weights = lax.linalg.triangular_solve(
        factor, middle, left_side=True, lower=True, transpose_a=True
    )
    return eye + weights - jnp.mean(weights, axis=0, keepdims=True)


def shards(
    present_ensemble,
    delayed_ensemble,
    spreading_coefficient,
    transport_ratios,
    obs_value,
    obs_error,
    obs_noise,
    obs_row,
    obs_col,
    obs_field,
):
    rows_here = present_ensemble.shape[2]
    row_start = lax.axis_index("slab") * rows_here
    predictive_dynamics = propagate_ahead(present_ensemble, spreading_coefficient, transport_ratios)
    flattened_system_array = jnp.concatenate(
        [predictive_dynamics[:, None], delayed_ensemble], axis=1
    )
    batch_count = obs_row.shape[0]
    columns = lax.all_to_all(flattened_system_array, "mem", split_axis=4, concat_axis=0, tiled=True)
    col_start = lax.axis_index("mem") * columns.shape[4]
    for batch in range(batch_count):
        partial_obs = observe(
            columns[:, 0], obs_row[batch], obs_col[batch], obs_field[batch], row_start, col_start
        )
        observed = lax.psum(partial_obs, ("slab", "mem"))
        matrix = transform(observed, obs_value[batch], obs_error[batch], obs_noise[batch])
        columns = jnp.einsum("jlfrn,jm->mlfrn", columns, matrix, precision=lax.Precision.HIGHEST)
    return lax.all_to_all(columns, "mem", split_axis=0, concat_axis=4, tiled=True)


def solution(mesh):
    return jax.shard_map(
        shards,
        mesh=mesh,
        in_specs=(
            P("mem", None, "slab", None),
            P("mem", None, None, "slab", None),
            P("slab", None),
            P(None, "slab", None),
            P(),
            P(),
            P(),
            P(),
            P(),
            P(),
        ),
        out_specs=P("mem", None, None, "slab", None),
        check_vma=False,
    )
```

profile of v0, /device:TPU:1, one launch (start us, length us, event | category | flops | bytes accessed | tf_op | source)
XLA Modules:
  0.0 1024.3 jit_solution(14442951278854169686)
XLA Ops:
  6.5 0.9 copy.140
  7.5 1.3 collective-permute-start
  8.8 4.7 collective-permute-start.1
  13.4 0.8 clamp_add_fusion.2
  14.2 0.8 clamp_add_fusion.1
  15.0 0.6 compare_and_fusion.5
  15.6 0.6 compare_and_fusion.7
  16.2 0.8 compare_and_fusion
  17.0 0.6 compare_and_fusion.2
  17.6 2.6 copy.142
  20.2 0.7 fusion.52
  20.9 1.5 fusion.51
  22.4 0.6 pad_clamp_fusion.5
  23.0 1.3 fusion.54
  24.3 1.3 fusion.53
  25.6 0.5 compare_select_fusion.2
  26.2 1.4 and_reduce_fusion.5
  27.8 1.3 copy.141
  29.2 2.7 fusion.57
  31.8 4.3 reshape.204
  36.1 10.0 all-to-all-start
  46.2 0.6 compare_and_fusion.4
  46.8 5.3 all-to-all-done
  52.1 0.5 broadcast.348
  52.6 1.0 reduce.16
  53.6 3.7 reshape.205
  57.3 1.5 copy.166
  59.0 0.7 gather_fusion.2
  59.7 0.7 gather_fusion.1
  60.4 0.9 gather_fusion
  61.4 1.6 fusion.11
  63.3 0.6 pad_clamp_fusion.2
  63.9 0.9 copy.170
  64.8 455.5 %all-reduce.4.cloned.1.call-done = f32[64,256]{0,1:T(8,128)} async-done(((f32[64,256]{0,1:T(8,128)}), f32[64,256]{0,1:T(8,128)}) %all-reduce.4.cloned.1.call-update) | async-done | bytes 65552 | tf_op jit(solution)/shard_map/psum | solution.py:110
  520.4 1.0 reduce_sum.36
  521.4 1.5 convolution_add_fusion.1
  523.1 5.8 cholesky.44
  528.9 0.6 compare_reduce_fusion.1
  529.6 0.7 fusion.29
  530.3 4.9 custom-call.11
  535.2 1.5 fusion.9
  536.7 0.2 fusion.42
  537.2 0.5 fusion
  537.9 0.7 gather_fusion.5
  538.6 0.7 gather_fusion.4
  539.3 0.7 gather_fusion.3
  540.1 0.9 fusion.5
  541.2 446.9 %all-reduce.6.cloned.1.call-done = f32[64,256]{0,1:T(8,128)} async-done(((f32[64,256]{0,1:T(8,128)}), f32[64,256]{0,1:T(8,128)}) %all-reduce.6.cloned.1.call-update) | async-done | bytes 65552 | tf_op jit(solution)/shard_map/psum | solution.py:110
  988.0 1.0 reduce_sum.38
  989.1 1.5 convolution_add_fusion
  990.7 5.8 cholesky.55
  996.6 0.6 compare_reduce_fusion
  997.2 0.7 fusion.30
  997.9 4.9 custom-call.13
  1002.8 1.5 fusion.3
  1004.4 0.2 fusion.37
  1004.9 0.5 convolution_bitcast_fusion
  1005.4 0.3 copy.174
  1005.7 0.4 reshape.206
  1006.0 9.0 all_to_all.36
  1015.1 1.0 reduce.17
  1016.1 0.3 reshape.207
  1016.3 0.2 copy.160
  1016.6 0.9 all_to_all.33
  (62 shorter events, 1.7 us)
Async XLA Ops:
  6.5 21.2 %copy-start = (f32[8,4,1,512]{3,2,1,0:T(1,128)S(1)}, f32[8,4,1,512]{3,2,1,0:T(1,128)}, u32[]{:S(2)}) copy-start(f32[8,4,1,512]{3,2,1,0:T(1,128)} %param.17) | copy-start | bytes 196612
  6.5 21.2 %copy-start.2 = (f32[1,512]{1,0:T(1,128)S(1)}, f32[1,512]{1,0:T(1,128)}, u32[]{:S(2)}) copy-start(f32[1,512]{1,0:T(1,128)} %param.19) | copy-start | bytes 6148
  7.5 20.1 %collective-permute-start = (f32[8,4,1,512]{3,0,2,1:T(8,128)S(1)}, f32[8,4,1,512]{3,0,2,1:T(8,128)S(1)}, u32[]{:S(2)}, u32[]{:S(2)}) collective-permute-start(f32[8,4,1,512]{3,0,2,1:T(8,128)S(1)} %copy.140), channel_id=1, source_target_pairs={{8,0},{16,8},{24,16},{32,24},{40,32},{48,40},{56,48},{64,56},{72,6... | collective-permute-start | bytes 196616 | tf_op jit(solution)/shard_map/ppermute | solution.py:15
  8.8 18.8 %collective-permute-start.1 = (f32[8,4,1,512]{3,0,2,1:T(8,128)S(1)}, f32[8,4,1,512]{3,0,2,1:T(8,128)S(1)}, u32[]{:S(2)}, u32[]{:S(2)}) collective-permute-start(f32[8,4,1,512]{3,0,2,1:T(8,128)S(1)} %copy.140), channel_id=1, source_target_pairs={{0,8},{8,16},{16,24},{24,32},{32,40},{40,48},{48,56},{56,64},{64,7... | collective-permute-start | bytes 196616 | tf_op jit(solution)/shard_map/ppermute | solution.py:14
  36.1 15.9 %all-to-all-start = ((f32[8,1,6144]{2,1,0:T(1,128)}), f32[8,1,6144]{2,1,0:T(1,128)S(1)}, u32[]{:S(2)}, u32[]{:S(2)}) async-start(f32[8,1,6144]{2,1,0:T(1,128)} %reshape.204), calls=%async_computation | async-start | bytes 393216 | tf_op jit(solution)/shard_map/all_to_all | solution.py:104
  46.2 474.2 %all-reduce.4.cloned.1.call-start = ((), (), s32[]{:S(2)}) async-start(), calls=%async_computation.2 | async-start | bytes 262144 | tf_op jit(solution)/shard_map/psum | solution.py:110
  58.9 462.6 %copy-start.11 = (f32[1,256]{1,0:T(1,128)S(1)}, f32[1,256]{1,0:T(1,128)}, u32[]{:S(2)}) copy-start(f32[1,256]{1,0:T(1,128)} %get-tuple-element.33) | copy-start | bytes 3076
  58.9 476.3 %copy-start.10 = (f32[1,256]{1,0:T(1,128)S(1)}, f32[1,256]{1,0:T(1,128)}, u32[]{:S(2)}) copy-start(f32[1,256]{1,0:T(1,128)} %get-tuple-element.35) | copy-start | bytes 3076
  61.3 478.8 %copy-start.3 = (pred[256]{0:T(512)(128)(4,1)S(1)}, pred[256]{0:T(512)(128)(4,1)}, u32[]{:S(2)}) copy-start(pred[256]{0:T(512)(128)(4,1)} %get-tuple-element.46) | copy-start | bytes 772
  61.3 478.8 %copy-start.4 = (pred[256]{0:T(512)(128)(4,1)S(1)}, pred[256]{0:T(512)(128)(4,1)}, u32[]{:S(2)}) copy-start(pred[256]{0:T(512)(128)(4,1)} %get-tuple-element.47) | copy-start | bytes 772
  61.3 478.8 %copy-start.5 = (pred[256]{0:T(512)(128)(4,1)S(1)}, pred[256]{0:T(512)(128)(4,1)}, u32[]{:S(2)}) copy-start(pred[256]{0:T(512)(128)(4,1)} %get-tuple-element.6) | copy-start | bytes 772
  61.3 478.8 %copy-start.6 = (pred[256]{0:T(512)(128)(4,1)S(1)}, pred[256]{0:T(512)(128)(4,1)}, u32[]{:S(2)}) copy-start(pred[256]{0:T(512)(128)(4,1)} %get-tuple-element.8) | copy-start | bytes 772
  61.4 478.8 %copy-start.7 = (pred[256]{0:T(512)(128)(4,1)S(1)}, pred[256]{0:T(512)(128)(4,1)}, u32[]{:S(2)}) copy-start(pred[256]{0:T(512)(128)(4,1)} %get-tuple-element.10) | copy-start | bytes 772
  61.4 478.8 %copy-start.12 = (pred[256]{0:T(512)(128)(4,1)S(1)}, pred[256]{0:T(512)(128)(4,1)}, u32[]{:S(2)}) copy-start(pred[256]{0:T(512)(128)(4,1)} %compare_and_fusion.4) | copy-start | bytes 772
  63.0 478.1 %copy-start.1 = (f32[1,64,256]{2,1,0:T(8,128)S(1)}, f32[1,64,256]{2,1,0:T(8,128)}, u32[]{:S(2)}) copy-start(f32[1,64,256]{2,1,0:T(8,128)} %get-tuple-element.22) | copy-start | bytes 196612
  63.0 925.0 %all-reduce.6.cloned.1.call-start = ((), (), s32[]{:S(2)}) async-start(), calls=%async_computation.3 | async-start | bytes 262144 | tf_op jit(solution)/shard_map/psum | solution.py:110
  521.4 467.7 %copy-start.9 = (f32[1,256]{1,0:T(1,128)S(1)}, f32[1,256]{1,0:T(1,128)}, u32[]{:S(2)}) copy-start(f32[1,256]{1,0:T(1,128)} %get-tuple-element.32) | copy-start | bytes 3076
  530.3 472.6 %copy-start.8 = (f32[1,256]{1,0:T(1,128)S(1)}, f32[1,256]{1,0:T(1,128)}, u32[]{:S(2)}) copy-start(f32[1,256]{1,0:T(1,128)} %get-tuple-element.34) | copy-start | bytes 3076
Sparse Core Ops, SparseCore 0:
  63.1 457.1 all-reduce.3
  541.2 446.7 all-reduce.5
where the time goes:
time: 1030 us; the launch traced here: 1020 us
  waiting for transfers between devices  908 us (88%)
  other arithmetic  41.6 us (4%)
  local copies, waits for them, and re-layouts  27.9 us (3%)
  starting transfers between devices  16.2 us (2%)
  between operations  13.9 us (1%)
    psum x2, waiting for transfers between devices, shards(): observed = lax.psum(partial_obs, ('slab', 'mem'))  902 us
  transfers between devices with their start and end apart: 5, of which 3 were waited for; matrix products, arithmetic and copies ran while one was open for 2% of the time, Pallas kernels for 0%

commit v1 on v0

v1 whole, which is shorter than its diff:
```python
import functools

import jax
import jax.numpy as jnp
from jax import lax
from jax.experimental import pallas as pl
from jax.experimental.pallas import tpu as pltpu
from jax.sharding import PartitionSpec as P

NY = 4
NC = 2
HIGHEST = lax.Precision.HIGHEST
F32 = jnp.float32
MESH = pl.DeviceIdType.MESH


def sides(x):
    rows = x.shape[0]
    row = lax.broadcasted_iota(jnp.int32, x.shape, 0) % 4
    lane = lax.broadcasted_iota(jnp.int32, x.shape, 1)
    left = pltpu.roll(x, 1, 1)
    right = pltpu.roll(x, 127, 1)
    before = jnp.where(row == 0, 0.0, pltpu.roll(left, 1, 0))
    after = jnp.where(row == 3, 0.0, pltpu.roll(right, rows - 1, 0))
    return jnp.where(lane == 0, before, left), jnp.where(lane == 127, after, right)


def gather_kernel(
    slabs,
    mems,
    cur_ref,
    delayed_ref,
    spread_ref,
    ratio_ref,
    row_ref,
    col_ref,
    field_ref,
    obs_ref,
    state_ref,
    above_ref,
    below_ref,
    fore_ref,
    smooth_ref,
    part_ref,
    ybuf,
    ysum,
    zbuf,
    zsum,
    own_ref,
    send_sem,
    recv_sem,
    local_sem,
):
    nz, nx = slabs // NY, mems // NC
    slab, mem = lax.axis_index("slab"), lax.axis_index("mem")
    z, y = slab // NY, slab % NY
    xc, core = mem // NC, mem % NC
    members, depth = cur_ref.shape[0], cur_ref.shape[1]
    rows = members * depth

    nxt = (lax.rem(slab + 1, slabs), mem)
    prv = (lax.rem(slab + slabs - 1, slabs), mem)
    ypeer = [(z * NY + lax.rem(y + d, NY), mem) for d in range(NY)]
    zpeer = [(lax.rem(z + d, nz) * NY + y, mem) for d in range(nz)]
    mpeer = [(slab, lax.rem(mem + d, mems)) for d in range(mems)]
    xpeer = [(slab, lax.rem(xc + d, nx) * NC + core) for d in range(nx)]
    twin = (slab, xc * NC + (1 - core))

    barrier = pltpu.get_barrier_semaphore()
    greeted = [nxt, prv] + ypeer[1:] + zpeer[1:] + mpeer[1:]
    for peer in greeted:
        pl.semaphore_signal(barrier, inc=1, device_id=peer, device_id_type=MESH)
    pl.semaphore_wait(barrier, len(greeted))

    used = [0]

    def send(src, dst, peer):
        k = used[0]
        used[0] += 1
        copy = pltpu.make_async_remote_copy(
            src_ref=src,
            dst_ref=dst,
            send_sem=send_sem.at[k],
            recv_sem=recv_sem.at[k],
            device_id=peer,
            device_id_type=MESH,
        )
        copy.start()
        return copy

    halo = [send(cur_ref, above_ref, nxt), send(cur_ref, below_ref, prv)]
    lagged = pl.ds(depth, delayed_ref.shape[1])
    level0 = pl.ds(0, depth)
    bulk = [send(delayed_ref, state_ref.at[mem, :, lagged, :], xpeer[d]) for d in range(1, nx)]
    keep = pltpu.make_async_copy(delayed_ref, state_ref.at[mem, :, lagged, :], local_sem.at[0])
    keep.start()

    cur = cur_ref[...].reshape(rows, 128)
    left, right = sides(cur)

    def every(c):
        block = jnp.concatenate([c] * (depth // 4), axis=0)
        return jnp.broadcast_to(block[None], (members, depth, 128)).reshape(rows, 128)

    spread = every(spread_ref[...])
    ratio0 = every(ratio_ref[0])
    ratio1 = every(ratio_ref[1])
    for copy in halo:
        copy.wait_recv()
    above = jnp.where(slab > 0, above_ref[...].reshape(rows, 128), 0.0)
    below = jnp.where(slab < slabs - 1, below_ref[...].reshape(rows, 128), 0.0)
    forecast = (
        cur
        + spread * (below + above + right + left - 4.0 * cur)
        - ratio0 * (below - above) * 0.5
        - ratio1 * (right - left) * 0.5
    )
    fore_ref[...] = forecast.reshape(members, depth, 128)
    for d in range(1, nx):
        bulk.append(send(fore_ref, state_ref.at[mem, :, level0, :], xpeer[d]))
    keep0 = pltpu.make_async_copy(fore_ref, state_ref.at[mem, :, level0, :], local_sem.at[1])
    keep0.start()

    left, right = sides(forecast)
    smooth = 0.25 * left + 0.5 * forecast + 0.25 * right
    smooth_ref[...] = smooth.reshape(members, depth, 128)
    place = jnp.where(row_ref[...] == slab, field_ref[...] * 512 + col_ref[...], -1)
    place = jnp.concatenate([place[b : b + 1] for b in range(place.shape[0])], axis=1)
    total = place.shape[1]
    spot = lax.broadcasted_iota(jnp.int32, (256, total), 0)
    acc = jnp.zeros((3 * members, total), F32)
    for g in range(depth // 2):
        values = jnp.concatenate([smooth_ref[:, 2 * g, :], smooth_ref[:, 2 * g + 1, :]], axis=1)
        high = values.astype(jnp.bfloat16).astype(F32)
        rest = values - high
        middle = rest.astype(jnp.bfloat16).astype(F32)
        low = rest - middle
        lhs = jnp.concatenate([high, middle, low], axis=0).astype(jnp.bfloat16)
        hot = jnp.where(spot + 256 * g == place, 1.0, 0.0).astype(jnp.bfloat16)
        acc = acc + jnp.dot(lhs, hot, preferred_element_type=F32)
    picked = acc[:members] + acc[members : 2 * members] + acc[2 * members :]
    for q in range(NY):
        part_ref[q] = picked[:, q * 128 : (q + 1) * 128]

    ysend = [send(part_ref.at[lax.rem(y + d, NY)], ybuf.at[d], ypeer[d]) for d in range(1, NY)]
    value = part_ref[y]
    for d, copy in enumerate(ysend, 1):
        copy.wait_recv()
        value = value + ybuf[d]
    ysum[...] = value

    zsend = [send(ysum, zbuf.at[d], zpeer[d]) for d in range(1, nz)]
    keep.wait()
    keep0.wait()
    for copy in bulk:
        copy.wait_recv()
    forward = []
    for d in range(nx):
        block = state_ref.at[lax.rem(xc + d, nx) * NC + core]
        forward.append(send(block, block, twin))

    for d, copy in enumerate(zsend, 1):
        copy.wait_recv()
        value = value + zbuf[d]
    zsum[...] = value
    own_ref[y] = value
    gathered = [send(zsum, own_ref.at[y], ypeer[d]) for d in range(1, NY)]
    for copy in gathered:
        copy.wait_recv()
    last = [send(own_ref, obs_ref.at[mem], mpeer[d]) for d in range(1, mems)]
    obs_ref[mem] = own_ref[...]
    for copy in last:
        copy.wait_recv()
    for copy in forward:
        copy.wait_recv()
    for copy in halo + bulk + ysend + zsend + forward + gathered + last:
        copy.wait_send()


def eliminate(system, n):
    row = lax.broadcasted_iota(jnp.int32, system.shape, 0)
    panel = 4
    for base in range(0, n, panel):
        columns = [
            jnp.broadcast_to(system[:, n + base + i : n + base + i + 1], system.shape)
            for i in range(panel)
        ]
        for i in range(panel):
            k = base + i
            mine = row == k
            column = columns[i]
            inverse = 1.0 / column[k : k + 1, :]
            pivot = system[k : k + 1, :] * inverse
            system = jnp.where(mine, pivot, system - column * pivot)
            for j in range(i + 1, panel):
                scale = columns[j][k : k + 1, :] * inverse
                columns[j] = jnp.where(mine, scale, columns[j] - column * scale)
    return system[:, :n]


def update_kernel(value_ref, error_ref, noise_ref, obs_ref, state_ref, out_ref, matrix_ref):
    mems, pieces, members, width = obs_ref.shape
    n = mems * members
    batches = value_ref.shape[0]
    per = pieces // batches
    eye = jnp.where(
        lax.broadcasted_iota(jnp.int32, (n, n), 0) == lax.broadcasted_iota(jnp.int32, (n, n), 1),
        1.0,
        0.0,
    )
    shifted = jnp.where(
        lax.broadcasted_iota(jnp.int32, (n, 2 * n), 0) + n
        == lax.broadcasted_iota(jnp.int32, (n, 2 * n), 1),
        n - 1.0,
        0.0,
    )
    so_far = None
    for b in range(batches):
        observed = jnp.concatenate(
            [obs_ref[:, q].reshape(n, width) for q in range(b * per, (b + 1) * per)], axis=1
        )
        if so_far is not None:
            observed = jnp.dot(so_far, observed, precision=HIGHEST, preferred_element_type=F32)
        error = error_ref[b : b + 1, :]
        scaled = (observed - jnp.mean(observed, axis=0, keepdims=True)) / error
        innovation = (value_ref[b : b + 1, :] - observed) / error + noise_ref[b]
        both = jnp.concatenate([innovation, scaled], axis=0)
        system = shifted + lax.dot_general(
            scaled, both, (((1,), (1,)), ((), ())), precision=HIGHEST, preferred_element_type=F32
        )
        weights = eliminate(system, n)
        matrix = (eye + weights - jnp.mean(weights, axis=0, keepdims=True)).T
        if so_far is None:
            so_far = matrix
        else:
            so_far = jnp.dot(matrix, so_far, precision=HIGHEST, preferred_element_type=F32)
    matrix_ref[...] = so_far
    start = pl.multiple_of(lax.axis_index("mem") * members, members)
    mine = matrix_ref[pl.ds(start, members), :]
    for t in range(0, state_ref.shape[2], 2):
        block = jnp.concatenate(
            [state_ref[:, :, t + i, :].reshape(n, 128) for i in range(2)], axis=1
        )
        result = jnp.dot(mine, block, precision=HIGHEST, preferred_element_type=F32)
        for i in range(2):
            out_ref[:, t + i, :] = result[:, i * 128 : (i + 1) * 128]


def shards(
    slabs,
    mems,
    present_ensemble,
    delayed_ensemble,
    spreading_coefficient,
    transport_ratios,
    obs_value,
    obs_error,
    obs_noise,
    obs_row,
    obs_col,
    obs_field,
):
    members, fields = present_ensemble.shape[:2]
    lags = delayed_ensemble.shape[1]
    depth = fields * 4
    levels = (lags + 1) * depth
    copies = 2 + 2 * (mems // NC - 1) + 2 * (NY - 1) + (slabs // NY - 1) + mems // NC + mems - 1
    vmem = pl.BlockSpec(memory_space=pltpu.VMEM)
    observed, state = pl.pallas_call(
        functools.partial(gather_kernel, slabs, mems),
        out_shape=(
            jax.ShapeDtypeStruct((mems, NY, members, 128), F32),
            jax.ShapeDtypeStruct((mems, members, levels, 128), F32),
        ),
        in_specs=[vmem] * 7,
        out_specs=(vmem, vmem),
        scratch_shapes=[
            pltpu.VMEM((members, depth, 128), F32),
            pltpu.VMEM((members, depth, 128), F32),
            pltpu.VMEM((members, depth, 128), F32),
            pltpu.VMEM((members, depth, 128), F32),
            pltpu.VMEM((NY, members, 128), F32),
            pltpu.VMEM((NY, members, 128), F32),
            pltpu.VMEM((members, 128), F32),
            pltpu.VMEM((slabs // NY, members, 128), F32),
            pltpu.VMEM((members, 128), F32),
            pltpu.VMEM((NY, members, 128), F32),
            pltpu.SemaphoreType.DMA((copies,)),
            pltpu.SemaphoreType.DMA((copies,)),
            pltpu.SemaphoreType.DMA((2,)),
        ],
        compiler_params=pltpu.CompilerParams(collective_id=0, has_side_effects=True),
        name="gather",
    )(
        present_ensemble.reshape(members, depth, 128),
        delayed_ensemble.reshape(members, lags * depth, 128),
        spreading_coefficient.reshape(4, 128),
        transport_ratios.reshape(2, 4, 128),
        obs_row,
        obs_col,
        obs_field,
    )
    result = pl.pallas_call(
        update_kernel,
        out_shape=jax.ShapeDtypeStruct((members, levels, 128), F32),
        in_specs=[vmem] * 5,
        out_specs=vmem,
        scratch_shapes=[pltpu.VMEM((mems * members, mems * members), F32)],
        name="update",
    )(obs_value, obs_error, obs_noise, observed, state)
    return result.reshape(members, lags + 1, fields, 1, 512)


def solution(mesh):
    slabs, mems = mesh.shape["slab"], mesh.shape["mem"]
    return jax.shard_map(
        functools.partial(shards, slabs, mems),
        mesh=mesh,
        in_specs=(
            P("mem", None, "slab", None),
            P("mem", None, None, "slab", None),
            P("slab", None),
            P(None, "slab", None),
            P(),
            P(),
            P(),
            P(),
            P(),
            P(),
        ),
        out_specs=P("mem", None, None, "slab", None),
        check_vma=False,
    )
```

time: 1030 us -> 53.6 us (0.05)
  waiting for transfers between devices: 908 us -> 0 us
  Pallas kernels: 0 us -> 53.4 us
  other arithmetic: 41.6 us -> 0 us
  local copies, waits for them, and re-layouts: 27.9 us -> 0 us
  starting transfers between devices: 16.2 us -> 0 us
  between operations: 13.9 us -> 0.01 us
    psum x2 -> x0, waiting for transfers between devices: 902 us -> none  [shards(): observed = lax.psum(partial_obs, ('slab', 'mem'))]
    pallas_call x0 -> x2, Pallas kernels: none -> 53.4 us  [the longest x1 44.1 us: shards(): pl.pallas_call(functools.partial(gather_kernel, slabs, mems), out_shape=(...]
    another operation x10 -> x0, other arithmetic: 24.1 us -> none  [the longest x6 13 us: transform(): factor = jnp.linalg.cholesky(system)]
    unnamed x34 -> x0, local copies, waits for them, and re-layouts: 13.3 us -> none
  transfers between devices with their start and end apart: 5 -> 0, of which waited for: 3 -> 0; matrix products, arithmetic and copies ran while one was open for 2% -> 0% of each run, Pallas kernels for 0% -> 0%
where the time goes in v1:
time: 53.6 us; the launch traced here: 53.5 us
  Pallas kernels  53.4 us (100%)
    pallas_call x1, Pallas kernels, shards(): pl.pallas_call(functools.partial(gather_kernel, slabs, mems), out_shape=(...  44.1 us
    pallas_call x1, Pallas kernels, shards(): pl.pallas_call(update_kernel, out_shape=jax.ShapeDtypeStruct((members, le...  9.34 us

profile of v1, /device:TPU:1, one launch (start us, length us, event | category | flops | bytes accessed | tf_op | source)
XLA Modules:
  0.0 53.5 jit_solution(12679365369075795845)
XLA Ops:
  0.0 44.1 %gather.1 = (f32[8,4,8,128]{3,2,1,0:T(8,128)}, f32[8,8,48,128]{3,2,1,0:T(8,128)}) custom-call(f32[8,16,128]{2,1,0:T(8,128)} %bitcast.6, f32[8,32,128]{2,1,0:T(8,128)} %bitcast.5, f32[4,128]{1,0:T(4,128)} %bitcast.8, f32[2,4,128]{2,1,0:T(4,128)} %bitcast.7, s32[2,256]{1,0:T(2,128)} %row_ref.1, s32[2,256]{1,0:T(2,128)} %col_ref.1, s32[2,256]{1,0:T(2,128)} %field_ref.1), custom_call_target="tpu_custom_call" | custom-call | tf_op jit(solution)/shard_map/gather/pallas_call | solution.py:269
  44.1 9.3 %update.1 = f32[8,48,128]{2,1,0:T(8,128)} custom-call(f32[2,256]{1,0:T(2,128)} %value_ref.1, f32[2,256]{1,0:T(2,128)} %error_ref.1, f32[2,64,256]{2,1,0:T(8,128)} %noise_ref.1, f32[8,4,8,128]{3,2,1,0:T(8,128)} %get-tuple-element.7.obs_ref, f32[8,8,48,128]{3,2,1,0:T(8,128)} %get-tuple-element.8.state_ref), custom_call_target="tpu_custom_call" | custom-call | tf_op jit(solution)/shard_map/update/pallas_call | solution.py:303

commit v2 on v1

--- a/solution.py
+++ b/solution.py
@@ -46,7 +46,7 @@
     ysum,
     zbuf,
     zsum,
-    own_ref,
+    hot_ref,
     send_sem,
     recv_sem,
     local_sem,
@@ -62,14 +62,38 @@
     prv = (lax.rem(slab + slabs - 1, slabs), mem)
     ypeer = [(z * NY + lax.rem(y + d, NY), mem) for d in range(NY)]
     zpeer = [(lax.rem(z + d, nz) * NY + y, mem) for d in range(nz)]
-    mpeer = [(slab, lax.rem(mem + d, mems)) for d in range(mems)]
+    plane = [
+        (z * NY + lax.rem(y + dy, NY), lax.rem(xc + dx, nx) * NC + core)
+        for dx in range(nx)
+        for dy in range(NY)
+    ][1:]
     xpeer = [(slab, lax.rem(xc + d, nx) * NC + core) for d in range(nx)]
     twin = (slab, xc * NC + (1 - core))
 
     barrier = pltpu.get_barrier_semaphore()
-    greeted = [nxt, prv] + ypeer[1:] + zpeer[1:] + mpeer[1:]
+    greeted = [nxt, prv, twin] + zpeer[1:] + plane
     for peer in greeted:
         pl.semaphore_signal(barrier, inc=1, device_id=peer, device_id_type=MESH)
+    cur = cur_ref[...].reshape(rows, 128)
+    left, right = sides(cur)
+
+    def every(c):
+        block = jnp.concatenate([c] * (depth // 4), axis=0)
+        return jnp.broadcast_to(block[None], (members, depth, 128)).reshape(rows, 128)
+
+    spread = every(spread_ref[...])
+    ratio0 = every(ratio_ref[0])
+    ratio1 = every(ratio_ref[1])
+    inner = cur + spread * (right + left - 4.0 * cur) - ratio1 * (right - left) * 0.5
+    fore_ref[...] = inner.reshape(members, depth, 128)
+    from_below = spread - 0.5 * ratio0
+    from_above = spread + 0.5 * ratio0
+    place = jnp.where(row_ref[...] == slab, field_ref[...] * 512 + col_ref[...], -1)
+    place = jnp.concatenate([place[b : b + 1] for b in range(place.shape[0])], axis=1)
+    total = place.shape[1]
+    spot = lax.broadcasted_iota(jnp.int32, (256, total), 0)
+    for g in range(depth // 2):
+        hot_ref[g] = jnp.where(spot + 256 * g == place, 1.0, 0.0).astype(jnp.bfloat16)
     pl.semaphore_wait(barrier, len(greeted))
 
     used = [0]
@@ -95,26 +119,12 @@
     keep = pltpu.make_async_copy(delayed_ref, state_ref.at[mem, :, lagged, :], local_sem.at[0])
     keep.start()
 
-    cur = cur_ref[...].reshape(rows, 128)
-    left, right = sides(cur)
-
-    def every(c):
-        block = jnp.concatenate([c] * (depth // 4), axis=0)
-        return jnp.broadcast_to(block[None], (members, depth, 128)).reshape(rows, 128)
-
-    spread = every(spread_ref[...])
-    ratio0 = every(ratio_ref[0])
-    ratio1 = every(ratio_ref[1])
     for copy in halo:
         copy.wait_recv()
     above = jnp.where(slab > 0, above_ref[...].reshape(rows, 128), 0.0)
     below = jnp.where(slab < slabs - 1, below_ref[...].reshape(rows, 128), 0.0)
-    forecast = (
-        cur
-        + spread * (below + above + right + left - 4.0 * cur)
-        - ratio0 * (below - above) * 0.5
-        - ratio1 * (right - left) * 0.5
-    )
+    inner = fore_ref[...].reshape(rows, 128)
+    forecast = inner + from_below * below + from_above * above
     fore_ref[...] = forecast.reshape(members, depth, 128)
     for d in range(1, nx):
         bulk.append(send(fore_ref, state_ref.at[mem, :, level0, :], xpeer[d]))
@@ -124,10 +134,6 @@
     left, right = sides(forecast)
     smooth = 0.25 * left + 0.5 * forecast + 0.25 * right
     smooth_ref[...] = smooth.reshape(members, depth, 128)
-    place = jnp.where(row_ref[...] == slab, field_ref[...] * 512 + col_ref[...], -1)
-    place = jnp.concatenate([place[b : b + 1] for b in range(place.shape[0])], axis=1)
-    total = place.shape[1]
-    spot = lax.broadcasted_iota(jnp.int32, (256, total), 0)
     acc = jnp.zeros((3 * members, total), F32)
     for g in range(depth // 2):
         values = jnp.concatenate([smooth_ref[:, 2 * g, :], smooth_ref[:, 2 * g + 1, :]], axis=1)
@@ -136,8 +142,7 @@
         middle = rest.astype(jnp.bfloat16).astype(F32)
         low = rest - middle
         lhs = jnp.concatenate([high, middle, low], axis=0).astype(jnp.bfloat16)
-        hot = jnp.where(spot + 256 * g == place, 1.0, 0.0).astype(jnp.bfloat16)
-        acc = acc + jnp.dot(lhs, hot, preferred_element_type=F32)
+        acc = acc + jnp.dot(lhs, hot_ref[g], preferred_element_type=F32)
     picked = acc[:members] + acc[members : 2 * members] + acc[2 * members :]
     for q in range(NY):
         part_ref[q] = picked[:, q * 128 : (q + 1) * 128]
@@ -149,7 +154,8 @@
         value = value + ybuf[d]
     ysum[...] = value
 
-    zsend = [send(ysum, zbuf.at[d], zpeer[d]) for d in range(1, nz)]
+    far = sorted(range(1, nz), key=lambda d: -min(d, nz - d))
+    zsend = [send(ysum, zbuf.at[d], zpeer[d]) for d in far]
     keep.wait()
     keep0.wait()
     for copy in bulk:
@@ -159,21 +165,23 @@
         block = state_ref.at[lax.rem(xc + d, nx) * NC + core]
         forward.append(send(block, block, twin))
 
-    for d, copy in enumerate(zsend, 1):
+    for d, copy in reversed(list(zip(far, zsend))):
         copy.wait_recv()
         value = value + zbuf[d]
     zsum[...] = value
-    own_ref[y] = value
-    gathered = [send(zsum, own_ref.at[y], ypeer[d]) for d in range(1, NY)]
-    for copy in gathered:
-        copy.wait_recv()
-    last = [send(own_ref, obs_ref.at[mem], mpeer[d]) for d in range(1, mems)]
-    obs_ref[mem] = own_ref[...]
+    obs_ref[mem, y] = value
+    tiles = [send(zsum, obs_ref.at[mem, y], peer) for peer in plane]
+    for copy in tiles:
+        copy.wait_recv()
+    last = []
+    for d in range(nx):
+        block = obs_ref.at[lax.rem(xc + d, nx) * NC + core]
+        last.append(send(block, block, twin))
     for copy in last:
         copy.wait_recv()
     for copy in forward:
         copy.wait_recv()
-    for copy in halo + bulk + ysend + zsend + forward + gathered + last:
+    for copy in halo + bulk + ysend + zsend + forward + tiles + last:
         copy.wait_send()
 
 
@@ -198,7 +206,9 @@
     return system[:, :n]
 
 
-def update_kernel(value_ref, error_ref, noise_ref, obs_ref, state_ref, out_ref, matrix_ref):
+def update_kernel(value_ref, error_ref, noise_ref, obs_ref, state_hbm, out_ref, matrix_ref, state_ref, load_sem):
+    load = pltpu.make_async_copy(state_hbm, state_ref, load_sem)
+    load.start()
     mems, pieces, members, width = obs_ref.shape
     n = mems * members
     batches = value_ref.shape[0]
@@ -237,6 +247,7 @@
     matrix_ref[...] = so_far
     start = pl.multiple_of(lax.axis_index("mem") * members, members)
     mine = matrix_ref[pl.ds(start, members), :]
+    load.wait()
     for t in range(0, state_ref.shape[2], 2):
         block = jnp.concatenate(
             [state_ref[:, :, t + i, :].reshape(n, 128) for i in range(2)], axis=1
@@ -264,7 +275,8 @@
     lags = delayed_ensemble.shape[1]
     depth = fields * 4
     levels = (lags + 1) * depth
-    copies = 2 + 2 * (mems // NC - 1) + 2 * (NY - 1) + (slabs // NY - 1) + mems // NC + mems - 1
+    nx = mems // NC
+    copies = 2 + 2 * (nx - 1) + (NY - 1) + (slabs // NY - 1) + (NY * nx - 1) + 2 * nx
     vmem = pl.BlockSpec(memory_space=pltpu.VMEM)
     observed, state = pl.pallas_call(
         functools.partial(gather_kernel, slabs, mems),
@@ -273,7 +285,7 @@
             jax.ShapeDtypeStruct((mems, members, levels, 128), F32),
         ),
         in_specs=[vmem] * 7,
-        out_specs=(vmem, vmem),
+        out_specs=(vmem, pl.BlockSpec(memory_space=pl.ANY)),
         scratch_shapes=[
             pltpu.VMEM((members, depth, 128), F32),
             pltpu.VMEM((members, depth, 128), F32),
@@ -284,7 +296,7 @@
             pltpu.VMEM((members, 128), F32),
             pltpu.VMEM((slabs // NY, members, 128), F32),
             pltpu.VMEM((members, 128), F32),
-            pltpu.VMEM((NY, members, 128), F32),
+            pltpu.VMEM((depth // 2, 256, obs_row.size), jnp.bfloat16),
             pltpu.SemaphoreType.DMA((copies,)),
             pltpu.SemaphoreType.DMA((copies,)),
             pltpu.SemaphoreType.DMA((2,)),
@@ -303,9 +315,13 @@
     result = pl.pallas_call(
         update_kernel,
         out_shape=jax.ShapeDtypeStruct((members, levels, 128), F32),
-        in_specs=[vmem] * 5,
+        in_specs=[vmem] * 4 + [pl.BlockSpec(memory_space=pl.ANY)],
         out_specs=vmem,
-        scratch_shapes=[pltpu.VMEM((mems * members, mems * members), F32)],
+        scratch_shapes=[
+            pltpu.VMEM((mems * members, mems * members), F32),
+            pltpu.VMEM((mems, members, levels, 128), F32),
+            pltpu.SemaphoreType.DMA,
+        ],
         name="update",
     )(obs_value, obs_error, obs_noise, observed, state)
     return result.reshape(members, lags + 1, fields, 1, 512)

time: 53.6 us -> 51.1 us (0.953)
  Pallas kernels: 53.4 us -> 50.9 us
    pallas_call x1, Pallas kernels: 44.1 us -> 42.1 us  [shards(): pl.pallas_call(functools.partial(gather_kernel, slabs, mems), out_shape=(...]
where the time goes in v2:
time: 51.1 us; the launch traced here: 50.9 us
  Pallas kernels  50.9 us (100%)
    pallas_call x1, Pallas kernels, shards(): pl.pallas_call(functools.partial(gather_kernel, slabs, mems), out_shape=(...  42.1 us
    pallas_call x1, Pallas kernels, shards(): pl.pallas_call(update_kernel, out_shape=jax.ShapeDtypeStruct((members, le...  8.83 us

profile of v2, /device:TPU:1, one launch (start us, length us, event | category | flops | bytes accessed | tf_op | source)
XLA Modules:
  0.0 50.9 jit_solution(16586071968338604515)
XLA Ops:
  0.0 42.1 %gather.1 = (f32[8,4,8,128]{3,2,1,0:T(8,128)}, f32[8,8,48,128]{3,2,1,0:T(8,128)}) custom-call(f32[8,16,128]{2,1,0:T(8,128)} %bitcast.6, f32[8,32,128]{2,1,0:T(8,128)} %bitcast.5, f32[4,128]{1,0:T(4,128)} %bitcast.8, f32[2,4,128]{2,1,0:T(4,128)} %bitcast.7, s32[2,256]{1,0:T(2,128)} %row_ref.1, s32[2,256]{1,0:T(2,128)} %col_ref.1, s32[2,256]{1,0:T(2,128)} %field_ref.1), custom_call_target="tpu_custom_call" | custom-call | tf_op jit(solution)/shard_map/gather/pallas_call | solution.py:281
  42.1 8.8 %update.1 = f32[8,48,128]{2,1,0:T(8,128)} custom-call(f32[2,256]{1,0:T(2,128)} %value_ref.1, f32[2,256]{1,0:T(2,128)} %error_ref.1, f32[2,64,256]{2,1,0:T(8,128)} %noise_ref.1, f32[8,4,8,128]{3,2,1,0:T(8,128)} %get-tuple-element.7.obs_ref, f32[8,8,48,128]{3,2,1,0:T(8,128)} %get-tuple-element.8.state_hbm), custom_call_target="tpu_custom_call" | custom-call | tf_op jit(solution)/shard_map/update/pallas_call | solution.py:315

commit v3 on v2

--- a/solution.py
+++ b/solution.py
@@ -25,7 +25,7 @@
     return jnp.where(lane == 0, before, left), jnp.where(lane == 127, after, right)
 
 
-def gather_kernel(
+def window_kernel(
     slabs,
     mems,
     cur_ref,
@@ -35,8 +35,13 @@
     row_ref,
     col_ref,
     field_ref,
+    value_ref,
+    error_ref,
+    noise_ref,
+    out_ref,
     obs_ref,
     state_ref,
+    matrix_ref,
     above_ref,
     below_ref,
     fore_ref,
@@ -179,8 +184,10 @@
         last.append(send(block, block, twin))
     for copy in last:
         copy.wait_recv()
+    matrix_ref[...] = solve(value_ref, error_ref, noise_ref, obs_ref)
     for copy in forward:
         copy.wait_recv()
+    apply(mem, matrix_ref, state_ref, out_ref)
     for copy in halo + bulk + ysend + zsend + forward + tiles + last:
         copy.wait_send()
 
@@ -206,9 +213,7 @@
     return system[:, :n]
 
 
-def update_kernel(value_ref, error_ref, noise_ref, obs_ref, state_hbm, out_ref, matrix_ref, state_ref, load_sem):
-    load = pltpu.make_async_copy(state_hbm, state_ref, load_sem)
-    load.start()
+def solve(value_ref, error_ref, noise_ref, obs_ref):
     mems, pieces, members, width = obs_ref.shape
     n = mems * members
     batches = value_ref.shape[0]
@@ -244,15 +249,27 @@
             so_far = matrix
         else:
             so_far = jnp.dot(matrix, so_far, precision=HIGHEST, preferred_element_type=F32)
-    matrix_ref[...] = so_far
-    start = pl.multiple_of(lax.axis_index("mem") * members, members)
-    mine = matrix_ref[pl.ds(start, members), :]
-    load.wait()
-    for t in range(0, state_ref.shape[2], 2):
+    return so_far
+
+
+def split(x):
+    high = x.astype(jnp.bfloat16)
+    return high, (x - high.astype(F32)).astype(jnp.bfloat16)
+
+
+def apply(mem, matrix_ref, state_ref, out_ref):
+    mems, members, levels = state_ref.shape[:3]
+    n = mems * members
+    high, low = split(matrix_ref[pl.ds(pl.multiple_of(mem * members, members), members), :])
+    lhs = jnp.concatenate([high.astype(F32), low.astype(F32), high.astype(F32)], axis=1)
+    lhs = lhs.astype(jnp.bfloat16)
+    for t in range(0, levels, 2):
         block = jnp.concatenate(
             [state_ref[:, :, t + i, :].reshape(n, 128) for i in range(2)], axis=1
         )
-        result = jnp.dot(mine, block, precision=HIGHEST, preferred_element_type=F32)
+        high, low = split(block)
+        rhs = jnp.concatenate([high, high, low], axis=0)
+        result = jnp.dot(lhs, rhs, preferred_element_type=F32)
         for i in range(2):
             out_ref[:, t + i, :] = result[:, i * 128 : (i + 1) * 128]
 
@@ -278,15 +295,16 @@
     nx = mems // NC
     copies = 2 + 2 * (nx - 1) + (NY - 1) + (slabs // NY - 1) + (NY * nx - 1) + 2 * nx
     vmem = pl.BlockSpec(memory_space=pltpu.VMEM)
-    observed, state = pl.pallas_call(
-        functools.partial(gather_kernel, slabs, mems),
-        out_shape=(
-            jax.ShapeDtypeStruct((mems, NY, members, 128), F32),
-            jax.ShapeDtypeStruct((mems, members, levels, 128), F32),
-        ),
-        in_specs=[vmem] * 7,
-        out_specs=(vmem, pl.BlockSpec(memory_space=pl.ANY)),
+    n = mems * members
+    result = pl.pallas_call(
+        functools.partial(window_kernel, slabs, mems),
+        out_shape=jax.ShapeDtypeStruct((members, levels, 128), F32),
+        in_specs=[vmem] * 10,
+        out_specs=vmem,
         scratch_shapes=[
+            pltpu.VMEM((mems, NY, members, 128), F32),
+            pltpu.VMEM((mems, members, levels, 128), F32),
+            pltpu.VMEM((n, n), F32),
             pltpu.VMEM((members, depth, 128), F32),
             pltpu.VMEM((members, depth, 128), F32),
             pltpu.VMEM((members, depth, 128), F32),
@@ -302,7 +320,7 @@
             pltpu.SemaphoreType.DMA((2,)),
         ],
         compiler_params=pltpu.CompilerParams(collective_id=0, has_side_effects=True),
-        name="gather",
+        name="window",
     )(
         present_ensemble.reshape(members, depth, 128),
         delayed_ensemble.reshape(members, lags * depth, 128),
@@ -311,19 +329,10 @@
         obs_row,
         obs_col,
         obs_field,
+        obs_value,
+        obs_error,
+        obs_noise,
     )
-    result = pl.pallas_call(
-        update_kernel,
-        out_shape=jax.ShapeDtypeStruct((members, levels, 128), F32),
-        in_specs=[vmem] * 4 + [pl.BlockSpec(memory_space=pl.ANY)],
-        out_specs=vmem,
-        scratch_shapes=[
-            pltpu.VMEM((mems * members, mems * members), F32),
-            pltpu.VMEM((mems, members, levels, 128), F32),
-            pltpu.SemaphoreType.DMA,
-        ],
-        name="update",
-    )(obs_value, obs_error, obs_noise, observed, state)
     return result.reshape(members, lags + 1, fields, 1, 512)
 
 

time: 51.1 us -> 51.4 us (level)
  local copies, waits for them, and re-layouts: 0 us -> 1.62 us
  Pallas kernels: 50.9 us -> 49.6 us
    unnamed x0 -> x1, local copies, waits for them, and re-layouts: none -> 1.62 us
    pallas_call x2 -> x1, Pallas kernels: 50.9 us -> 49.6 us  [shards(): pl.pallas_call(functools.partial(window_kernel, slabs, mems), out_shape=j...]
where the time goes in v3:
time: 51.4 us; the launch traced here: 51.3 us
  Pallas kernels  49.6 us (96%)
  local copies, waits for them, and re-layouts  1.62 us (3%)
    pallas_call x1, Pallas kernels, shards(): pl.pallas_call(functools.partial(window_kernel, slabs, mems), out_shape=j...  49.6 us
    unnamed x1, local copies, waits for them, and re-layouts  1.62 us

profile of v3, /device:TPU:1, one launch (start us, length us, event | category | flops | bytes accessed | tf_op | source)
XLA Modules:
  0.0 51.3 jit_solution(91521419045734128)
XLA Ops:
  0.0 49.6 %window.1 = f32[8,48,128]{2,1,0:T(8,128)} custom-call(f32[8,16,128]{2,1,0:T(8,128)} %bitcast.7, f32[8,32,128]{2,1,0:T(8,128)} %bitcast.6, f32[4,128]{1,0:T(4,128)} %bitcast.9, f32[2,4,128]{2,1,0:T(4,128)} %bitcast.8, s32[2,256]{1,0:T(2,128)} %row_ref.1, s32[2,256]{1,0:T(2,128)} %col_ref.1, s32[2,256]{1,0:T(2,128)} %field_ref.1, f32[2,256]{1,0:T(2,128)} %value_ref.1, ...), custom_call_target="tpu_custom_call" | custom-call | tf_op jit(solution)/shard_map/window/pallas_call | solution.py:299
  49.6 1.6 %copy.13 = f32[8,3,4,1,512]{4,3,2,1,0:T(1,128)} copy(f32[8,3,4,1,512]{4,3,2,1,0:T(1,128)} %bitcast.5) | data formatting | bytes 393216

commit v4 on v2

--- a/solution.py
+++ b/solution.py
@@ -63,15 +63,15 @@
     ypeer = [(z * NY + lax.rem(y + d, NY), mem) for d in range(NY)]
     zpeer = [(lax.rem(z + d, nz) * NY + y, mem) for d in range(nz)]
     plane = [
-        (z * NY + lax.rem(y + dy, NY), lax.rem(xc + dx, nx) * NC + core)
-        for dx in range(nx)
+        (z * NY + lax.rem(y + dy, NY), lax.rem(mem + dm, mems))
+        for dm in range(mems)
         for dy in range(NY)
     ][1:]
     xpeer = [(slab, lax.rem(xc + d, nx) * NC + core) for d in range(nx)]
     twin = (slab, xc * NC + (1 - core))
 
     barrier = pltpu.get_barrier_semaphore()
-    greeted = [nxt, prv, twin] + zpeer[1:] + plane
+    greeted = [nxt, prv] + zpeer[1:] + plane
     for peer in greeted:
         pl.semaphore_signal(barrier, inc=1, device_id=peer, device_id_type=MESH)
     cur = cur_ref[...].reshape(rows, 128)
@@ -173,21 +173,15 @@
     tiles = [send(zsum, obs_ref.at[mem, y], peer) for peer in plane]
     for copy in tiles:
         copy.wait_recv()
-    last = []
-    for d in range(nx):
-        block = obs_ref.at[lax.rem(xc + d, nx) * NC + core]
-        last.append(send(block, block, twin))
-    for copy in last:
-        copy.wait_recv()
     for copy in forward:
         copy.wait_recv()
-    for copy in halo + bulk + ysend + zsend + forward + tiles + last:
+    for copy in halo + bulk + ysend + zsend + forward + tiles:
         copy.wait_send()
 
 
 def eliminate(system, n):
     row = lax.broadcasted_iota(jnp.int32, system.shape, 0)
-    panel = 4
+    panel = 8
     for base in range(0, n, panel):
         columns = [
             jnp.broadcast_to(system[:, n + base + i : n + base + i + 1], system.shape)
@@ -204,6 +198,11 @@
                 scale = columns[j][k : k + 1, :] * inverse
                 columns[j] = jnp.where(mine, scale, columns[j] - column * scale)
     return system[:, :n]
+
+
+def split(x):
+    high = x.astype(jnp.bfloat16)
+    return high, (x - high.astype(F32)).astype(jnp.bfloat16)
 
 
 def update_kernel(value_ref, error_ref, noise_ref, obs_ref, state_hbm, out_ref, matrix_ref, state_ref, load_sem):
@@ -247,12 +246,17 @@
     matrix_ref[...] = so_far
     start = pl.multiple_of(lax.axis_index("mem") * members, members)
     mine = matrix_ref[pl.ds(start, members), :]
+    high, low = split(mine)
+    lhs = jnp.concatenate([high.astype(F32), low.astype(F32), high.astype(F32)], axis=1)
+    lhs = lhs.astype(jnp.bfloat16)
     load.wait()
     for t in range(0, state_ref.shape[2], 2):
         block = jnp.concatenate(
             [state_ref[:, :, t + i, :].reshape(n, 128) for i in range(2)], axis=1
         )
-        result = jnp.dot(mine, block, precision=HIGHEST, preferred_element_type=F32)
+        high, low = split(block)
+        rhs = jnp.concatenate([high, high, low], axis=0)
+        result = jnp.dot(lhs, rhs, preferred_element_type=F32)
         for i in range(2):
             out_ref[:, t + i, :] = result[:, i * 128 : (i + 1) * 128]
 
@@ -276,7 +280,7 @@
     depth = fields * 4
     levels = (lags + 1) * depth
     nx = mems // NC
-    copies = 2 + 2 * (nx - 1) + (NY - 1) + (slabs // NY - 1) + (NY * nx - 1) + 2 * nx
+    copies = 2 + 2 * (nx - 1) + (NY - 1) + (slabs // NY - 1) + (NY * mems - 1) + nx
     vmem = pl.BlockSpec(memory_space=pltpu.VMEM)
     observed, state = pl.pallas_call(
         functools.partial(gather_kernel, slabs, mems),

time: 51.1 us -> 49.1 us (0.961)
  Pallas kernels: 50.9 us -> 48.9 us
    pallas_call x1, Pallas kernels: 8.83 us -> 7.57 us  [shards(): pl.pallas_call(update_kernel, out_shape=jax.ShapeDtypeStruct((members, le...]
    pallas_call x1, Pallas kernels: 42.1 us -> 41.4 us  [shards(): pl.pallas_call(functools.partial(gather_kernel, slabs, mems), out_shape=(...]
where the time goes in v4:
time: 49.1 us; the launch traced here: 49 us
  Pallas kernels  48.9 us (100%)
    pallas_call x1, Pallas kernels, shards(): pl.pallas_call(functools.partial(gather_kernel, slabs, mems), out_shape=(...  41.4 us
    pallas_call x1, Pallas kernels, shards(): pl.pallas_call(update_kernel, out_shape=jax.ShapeDtypeStruct((members, le...  7.57 us

profile of v4, /device:TPU:1, one launch (start us, length us, event | category | flops | bytes accessed | tf_op | source)
XLA Modules:
  0.0 49.0 jit_solution(8555214865806691182)
XLA Ops:
  0.0 41.4 %gather.1 = (f32[8,4,8,128]{3,2,1,0:T(8,128)}, f32[8,8,48,128]{3,2,1,0:T(8,128)}) custom-call(f32[8,16,128]{2,1,0:T(8,128)} %bitcast.6, f32[8,32,128]{2,1,0:T(8,128)} %bitcast.5, f32[4,128]{1,0:T(4,128)} %bitcast.8, f32[2,4,128]{2,1,0:T(4,128)} %bitcast.7, s32[2,256]{1,0:T(2,128)} %row_ref.1, s32[2,256]{1,0:T(2,128)} %col_ref.1, s32[2,256]{1,0:T(2,128)} %field_ref.1), custom_call_target="tpu_custom_call" | custom-call | tf_op jit(solution)/shard_map/gather/pallas_call | solution.py:285
  41.4 7.6 %update.1 = f32[8,48,128]{2,1,0:T(8,128)} custom-call(f32[2,256]{1,0:T(2,128)} %value_ref.1, f32[2,256]{1,0:T(2,128)} %error_ref.1, f32[2,64,256]{2,1,0:T(8,128)} %noise_ref.1, f32[8,4,8,128]{3,2,1,0:T(8,128)} %get-tuple-element.7.obs_ref, f32[8,8,48,128]{3,2,1,0:T(8,128)} %get-tuple-element.8.state_hbm), custom_call_target="tpu_custom_call" | custom-call | tf_op jit(solution)/shard_map/update/pallas_call | solution.py:319

commit v5 on v4

--- a/solution.py
+++ b/solution.py
@@ -181,7 +181,7 @@
 
 def eliminate(system, n):
     row = lax.broadcasted_iota(jnp.int32, system.shape, 0)
-    panel = 8
+    panel = 16
     for base in range(0, n, panel):
         columns = [
             jnp.broadcast_to(system[:, n + base + i : n + base + i + 1], system.shape)

time: 49.1 us -> 48.6 us (0.990)
  no operation moved by 1% of the time
where the time goes in v5:
time: 48.6 us; the launch traced here: 48.5 us
  Pallas kernels  48.5 us (100%)
    pallas_call x1, Pallas kernels, shards(): pl.pallas_call(functools.partial(gather_kernel, slabs, mems), out_shape=(...  41.4 us
    pallas_call x1, Pallas kernels, shards(): pl.pallas_call(update_kernel, out_shape=jax.ShapeDtypeStruct((members, le...  7.09 us

profile of v5, /device:TPU:1, one launch (start us, length us, event | category | flops | bytes accessed | tf_op | source)
XLA Modules:
  0.0 48.5 jit_solution(6876744580058333780)
XLA Ops:
  0.0 41.4 %gather.1 = (f32[8,4,8,128]{3,2,1,0:T(8,128)}, f32[8,8,48,128]{3,2,1,0:T(8,128)}) custom-call(f32[8,16,128]{2,1,0:T(8,128)} %bitcast.6, f32[8,32,128]{2,1,0:T(8,128)} %bitcast.5, f32[4,128]{1,0:T(4,128)} %bitcast.8, f32[2,4,128]{2,1,0:T(4,128)} %bitcast.7, s32[2,256]{1,0:T(2,128)} %row_ref.1, s32[2,256]{1,0:T(2,128)} %col_ref.1, s32[2,256]{1,0:T(2,128)} %field_ref.1), custom_call_target="tpu_custom_call" | custom-call | tf_op jit(solution)/shard_map/gather/pallas_call | solution.py:285
  41.4 7.1 %update.1 = f32[8,48,128]{2,1,0:T(8,128)} custom-call(f32[2,256]{1,0:T(2,128)} %value_ref.1, f32[2,256]{1,0:T(2,128)} %error_ref.1, f32[2,64,256]{2,1,0:T(8,128)} %noise_ref.1, f32[8,4,8,128]{3,2,1,0:T(8,128)} %get-tuple-element.7.obs_ref, f32[8,8,48,128]{3,2,1,0:T(8,128)} %get-tuple-element.8.state_hbm), custom_call_target="tpu_custom_call" | custom-call | tf_op jit(solution)/shard_map/update/pallas_call | solution.py:319
